TPU v7x, 32 devices: a whole 2x2x4 slice. The times are simulated.
32 devices in a mesh: groups: 2 (over y), wide: 4 (over z), narrow: 4 (over x, core).
Axes of the slice: x: 2, y: 2, z: 4, core: 2. Of those that a mesh axis runs over, the one named last changes fastest.
Arguments:
- tokens: bfloat16 [512, 4096], P(('groups', 'wide'), 'narrow'), parts along dimension 0, may hold values from -6 to 6
- routes: int32 [512, 8], P(('groups', 'wide')), parts along dimension 0, may hold values from 0 to 15, all different within a row; in each aligned block of 64 rows (0 to 63, 64 to 127, ...) at most 40 rows name the same one
- gate_weights: float32 [512, 8], P(('groups', 'wide')), parts along dimension 0, may hold values from 0.05 to 1
- delta_of: int32 [16], replicated, may hold values from 0 to 15, each once
- base_gate: bfloat16 [4096, 1536], P('wide', 'narrow'), may hold values from -0.09375 to 0.09375
- base_up: bfloat16 [4096, 1536], P('wide', 'narrow'), may hold values from -0.09375 to 0.09375
- base_down: bfloat16 [1536, 4096], P('wide', 'narrow'), may hold values from -0.15625 to 0.15625
- gate_left: bfloat16 [16, 4096, 32], P('wide', 'narrow'), may hold values from -0.09375 to 0.09375
- gate_right: bfloat16 [16, 32, 1536], P('wide', None, 'narrow'), may hold values from -0.5 to 0.5
- up_left: bfloat16 [16, 4096, 32], P('wide', 'narrow'), may hold values from -0.09375 to 0.09375
- up_right: bfloat16 [16, 32, 1536], P('wide', None, 'narrow'), may hold values from -0.5 to 0.5
- down_left: bfloat16 [16, 1536, 32], P('wide', 'narrow'), may hold values from -0.15625 to 0.15625
- down_right: bfloat16 [16, 32, 4096], P('wide', None, 'narrow'), may hold values from -0.5 to 0.5
Outputs:
- mixed_out: bfloat16 [512, 4096], P(('groups', 'wide'), 'narrow'), parts along dimension 0
There are 2 independent parts, one for each index of `groups`. A program takes and returns all parts, laid end to end along the dimension named above; an argument that names none is the same for every part. Nothing has to cross between parts.
Inputs may be any that keep to these rules, and one draw needn't show every extreme that they name: `routes`: in each aligned block of 64 rows (the rows of one index of wide) no expert is named by more than 40 rows, and in some block some expert is named by exactly 40 rows.
All inputs are finite; a program needn't handle non-finite values.
Results may differ from a plain program's by a relative error of at most 0.0053.
Values may be sent and summed in bfloat16 or wider, within the bound.
A program may use at most 64 MiB of HBM per device.

v0:
```python
import jax
import jax.numpy as jnp
from jax import lax
from jax.sharding import PartitionSpec as P


def dot32(a, b):
    return jnp.dot(a, b, preferred_element_type=jnp.float32)


def shards(
    tokens,
    routes,
    gate_weights,
    delta_of,
    base_gate,
    base_up,
    base_down,
    gate_left,
    gate_right,
    up_left,
    up_right,
    down_left,
    down_right,
):
    exp_here, _, rank = gate_left.shape
    experts = delta_of.shape[0]
    mine = lax.axis_index("wide")
    bf16 = jnp.bfloat16
    expert_ids = lax.broadcasted_iota(jnp.int32, (1, 1, experts), 2)
    named = routes[:, :, None] == expert_ids
    delta_ids = jnp.sum(jnp.where(named, delta_of[None, None, :], 0), axis=2)
    weight_of = jnp.sum(
        jnp.where(delta_ids[:, :, None] == expert_ids, gate_weights[:, :, None], 0.0), axis=1
    )
    weights = lax.all_gather(weight_of, "wide", axis=0, tiled=True)
    weights = lax.dynamic_slice_in_dim(weights, mine * exp_here, exp_here, axis=1)
    rows = lax.all_gather(tokens, "wide", axis=0, tiled=True)
    full = lax.all_gather(rows, "narrow", axis=1, tiled=True)
    depth = base_gate.shape[0]
    part = lax.dynamic_slice_in_dim(full, mine * depth, depth, axis=1)
    base_both = jnp.concatenate([base_gate, base_up], axis=1)
    both = lax.psum(dot32(part, base_both), "wide")
    columns = base_gate.shape[1]
    lefts = jnp.concatenate([gate_left, up_left], axis=0)
    low = lax.psum(
        jnp.einsum("td,edr->ter", rows, lefts, preferred_element_type=jnp.float32), "narrow"
    )
    low = low.astype(bf16)
    mixed = 0.0
    thin = []
    for e in range(exp_here):
        gate = both[:, :columns] + dot32(low[:, e], gate_right[e])
        up = both[:, columns:] + dot32(low[:, exp_here + e], up_right[e])
        hidden = jax.nn.silu(gate) * up * weights[:, e : e + 1]
        mixed = mixed + hidden
        thin.append(dot32(hidden.astype(bf16), down_left[e]))
    mixed = lax.psum(mixed, "wide").astype(bf16)
    mixed_full = lax.all_gather(mixed, "narrow", axis=1, tiled=True)
    depth = base_down.shape[0]
    mixed_part = lax.dynamic_slice_in_dim(mixed_full, mine * depth, depth, axis=1)
    thin = lax.psum(jnp.concatenate(thin, axis=1), "narrow").astype(bf16)
    out = dot32(mixed_part, base_down) + dot32(thin, down_right.reshape(exp_here * rank, -1))
    out = lax.psum_scatter(out, "wide", scatter_dimension=0, tiled=True)
    return out.astype(bf16)


def solution(mesh):
    return jax.shard_map(
        shards,
        mesh=mesh,
        in_specs=(
            P(("groups", "wide"), "narrow"),
            P(("groups", "wide"), None),
            P(("groups", "wide"), None),
            P(),
            P("wide", "narrow"),
            P("wide", "narrow"),
            P("wide", "narrow"),
            P("wide", "narrow", None),
            P("wide", None, "narrow"),
            P("wide", "narrow", None),
            P("wide", None, "narrow"),
            P("wide", "narrow", None),
            P("wide", None, "narrow"),
        ),
        out_specs=P(("groups", "wide"), "narrow"),
        check_vma=False,
    )
```

profile of v0, /device:TPU:0, one launch (start us, length us, event | category | flops | bytes accessed | tf_op | source)
XLA Modules:
  0.0 180.8 jit_solution(11253720552039283029)
XLA Ops:
  6.5 0.0 copy-start
  6.5 0.0 all-gather.3.cloned.1.call-start
  6.5 19.5 %all_gather.12 = bf16[256,1024]{1,0:T(8,128)(2,1)} all-gather(bf16[64,1024]{1,0:T(8,128)(2,1)} %param.13), channel_id=1, replica_groups=mesh['groups'=2,'wide'=4,'narrow'=4] {'wide'}, dimensions={0}, use_global_device_ids=true | all-gather | bytes 655360 | tf_op jit(solution)/shard_map/all_gather | solution.py:38
  26.0 0.0 all-gather.3.cloned.1.call-update
  26.0 0.0 all-reduce.5.cloned.1.call-start
  26.1 0.0 copy-start.2
  26.1 0.0 copy-start.10
  26.1 0.0 copy-start.11
  26.1 22.3 %all-gather.3.cloned.1.call-done = bf16[256,4096]{1,0:T(8,128)(2,1)} async-done(((bf16[256,1024]{1,0:T(8,128)(2,1)}), bf16[256,4096]{1,0:T(8,128)(2,1)}) %all-gather.3.cloned.1.call-update) | async-done | bytes 2097168 | tf_op jit(solution)/shard_map/all_gather | solution.py:39
  48.5 3.0 %fusion = f32[256,768]{1,0:T(8,128)} fusion(bf16[1024,384]{1,0:T(8,128)(2,1)} %param.18, bf16[1024,384]{1,0:T(8,128)(2,1)} %param.17, bf16[256,4096]{1,0:T(8,128)(2,1)} %all-gather.3.cloned.1.call-done, s32[]{:T(128)S(6)} %select_n.17), kind=kOutput, calls=%fused_computation | convolution fusion | flops 405798912 | bytes 2883588 | tf_op jit(solution)/shard_map/dot_general | solution.py:8
  51.5 0.0 copy-start.7
  51.5 0.0 copy-start.9
  51.5 0.0 copy-start.8
  51.5 0.0 copy-start.4
  51.5 0.0 copy-start.6
  51.5 0.0 all-reduce.5.cloned.1.call-update
  51.5 0.0 reduce-scatter.2.cloned.1.call-start
  51.6 0.0 copy-done.2
  51.6 0.0 copy-done.10
  51.6 0.0 copy-done.11
  51.6 0.3 convolution_bitcast_fusion
  52.0 0.2 copy-done.7
  52.2 0.0 copy-done.9
  52.2 0.0 copy-start.5
  52.2 0.1 select_reduce_fusion.1
  52.3 0.0 copy-done.8
  52.3 13.5 %all-gather = f32[4,64,16]{1,2,0:T(8,128)S(1)} all-gather(f32[1,64,16]{1,2,0:T(8,128)S(1)} %bitcast.82), channel_id=1, replica_groups=mesh['groups'=2,'wide'=4,'narrow'=4] {'wide'}, dimensions={0}, use_global_device_ids=true | all-gather | bytes 20480 | tf_op jit(solution)/shard_map/all_gather | solution.py:36
  65.8 0.1 reshape.9
  65.9 13.8 %all-reduce.6 = bf16[256,8,32]{0,2,1:T(8,128)(2,1)S(1)} all-reduce(f32[256,8,32]{0,2,1:T(8,128)S(1)} %convolution_bitcast_fusion), channel_id=1, replica_groups=mesh['groups'=2,'wide'=4,'narrow'=4] {'narrow'}, use_global_device_ids=true, to_apply=%region_1.2 | all-reduce | flops 65536 | bytes 393216 | tf_op jit(solution)/shard_map/psum | solution.py:46
  79.8 15.9 %all-reduce.5.cloned.1.call-done = f32[256,768]{1,0:T(8,128)} async-done(((f32[256,768]{1,0:T(8,128)}), f32[256,768]{1,0:T(8,128)}) %all-reduce.5.cloned.1.call-update) | async-done | bytes 786448 | tf_op jit(solution)/shard_map/psum | solution.py:43
  95.7 0.0 copy-done.4
  95.7 0.0 copy-start.1
  95.7 1.3 convolution_add_fusion.4
  97.0 0.0 copy-done.6
  97.0 1.3 fusion.10
  98.2 0.0 copy-done.5
  98.3 0.2 fusion.19
  98.4 0.0 copy-done.1
  98.4 0.2 convolution_add_fusion.6
  98.7 0.3 fusion.9
  99.0 0.2 fusion.21
  99.1 0.3 convolution_add_fusion.8
  99.4 0.3 fusion.8
  99.7 0.2 fusion.23
  99.9 0.3 convolution_add_fusion.2
  100.1 0.0 copy-start.3
  100.1 0.3 add_add_fusion
  100.5 0.2 fusion.17
  100.7 11.8 %all-reduce.7 = bf16[256,128]{0,1:T(8,128)(2,1)S(1)} all-reduce(f32[256,128]{0,1:T(8,128)S(1)} %pad_maximum_fusion), channel_id=1, replica_groups=mesh['groups'=2,'wide'=4,'narrow'=4] {'narrow'}, use_global_device_ids=true, to_apply=%region_5.6 | all-reduce | flops 32768 | bytes 196608 | tf_op jit(solution)/shard_map/psum | solution.py:62
  112.5 25.1 %all-reduce.8 = bf16[256,384]{1,0:T(8,128)(2,1)S(1)} all-reduce(f32[256,384]{1,0:T(8,128)S(1)} %get-tuple-element.9), channel_id=1, replica_groups=mesh['groups'=2,'wide'=4,'narrow'=4] {'wide'}, use_global_device_ids=true, to_apply=%region_4.5 | all-reduce | flops 98304 | bytes 589824 | tf_op jit(solution)/shard_map/psum | solution.py:58
  137.6 7.4 %all_gather.15 = bf16[256,1536]{1,0:T(8,128)(2,1)S(1)} all-gather(bf16[256,384]{1,0:T(8,128)(2,1)S(1)} %all-reduce.8), channel_id=1, replica_groups=mesh['groups'=2,'wide'=4,'narrow'=4] {'narrow'}, dimensions={1}, use_global_device_ids=true | all-gather | bytes 983040 | tf_op jit(solution)/shard_map/all_gather | solution.py:59
  145.0 0.0 copy-done.3
  145.0 0.3 fusion.56
  145.3 0.0 copy-done
  145.3 1.4 convolution_add_fusion
  146.7 0.0 reduce-scatter.2.cloned.1.call-update
  146.8 25.9 %reduce-scatter.2.cloned.1.call-done = f32[64,1024]{1,0:T(8,128)} async-done(((f32[256,1024]{1,0:T(8,128)}), f32[64,1024]{1,0:T(8,128)}) %reduce-scatter.2.cloned.1.call-update) | async-done | bytes 262160 | tf_op jit(solution)/shard_map/reduce_scatter | solution.py:64
  172.7 1.6 convert_element_type.31
  (4 shorter events, 0.1 us)
Async XLA Ops:
  6.5 138.8 %copy-start = (bf16[384,1024]{1,0:T(8,128)(2,1)S(1)}, bf16[384,1024]{1,0:T(8,128)(2,1)}, u32[]{:S(2)}) copy-start(bf16[384,1024]{1,0:T(8,128)(2,1)} %param.19) | copy-start | bytes 2359300
  6.5 41.9 %all-gather.3.cloned.1.call-start = ((), (), s32[]{:S(2)}) async-start(), calls=%async_computation.1 | async-start | bytes 2621440 | tf_op jit(solution)/shard_map/all_gather | solution.py:39
  26.0 69.6 %all-reduce.5.cloned.1.call-start = ((), (), s32[]{:S(2)}) async-start(), calls=%async_computation.2 | async-start | bytes 1572864 | tf_op jit(solution)/shard_map/psum | solution.py:43
  26.1 25.5 %copy-start.2 = (bf16[256,1024]{1,0:T(8,128)(2,1)S(1)}, bf16[256,1024]{1,0:T(8,128)(2,1)}, u32[]{:S(2)}) copy-start(bf16[256,1024]{1,0:T(8,128)(2,1)} %all_gather.12) | copy-start | bytes 1572868
  26.1 25.5 %copy-start.10 = (bf16[4,1024,32]{1,2,0:T(8,128)(2,1)S(1)}, bf16[4,1024,32]{1,2,0:T(8,128)(2,1)}, u32[]{:S(2)}) copy-start(bf16[4,1024,32]{1,2,0:T(8,128)(2,1)} %param.22) | copy-start | bytes 786436
  26.1 25.5 %copy-start.11 = (bf16[4,1024,32]{1,2,0:T(8,128)(2,1)S(1)}, bf16[4,1024,32]{1,2,0:T(8,128)(2,1)}, u32[]{:S(2)}) copy-start(bf16[4,1024,32]{1,2,0:T(8,128)(2,1)} %param.20) | copy-start | bytes 786436
  51.5 0.7 copy-start.7
  51.5 0.7 copy-start.9
  51.5 0.8 copy-start.8
  51.5 44.2 %copy-start.4 = (bf16[4,32,384]{2,1,0:T(8,128)(2,1)S(1)}, bf16[4,32,384]{2,1,0:T(8,128)(2,1)}, u32[]{:S(2)}) copy-start(bf16[4,32,384]{2,1,0:T(8,128)(2,1)} %param.21) | copy-start | bytes 294916
  51.5 45.5 %copy-start.6 = (bf16[4,32,384]{2,1,0:T(8,128)(2,1)S(1)}, bf16[4,32,384]{2,1,0:T(8,128)(2,1)}, u32[]{:S(2)}) copy-start(bf16[4,32,384]{2,1,0:T(8,128)(2,1)} %param.23) | copy-start | bytes 294916
  51.5 121.1 %reduce-scatter.2.cloned.1.call-start = ((), (), s32[]{:S(2)}) async-start(), calls=%async_computation.3 | async-start | bytes 1310720 | tf_op jit(solution)/shard_map/reduce_scatter | solution.py:64
  52.2 46.1 %copy-start.5 = (bf16[4,384,32]{1,2,0:T(8,128)(2,1)S(1)}, bf16[4,384,32]{1,2,0:T(8,128)(2,1)}, u32[]{:S(2)}) copy-start(bf16[4,384,32]{1,2,0:T(8,128)(2,1)} %param.24) | copy-start | bytes 294916
  95.7 2.8 %copy-start.1 = (f32[256,768]{1,0:T(8,128)S(1)}, f32[256,768]{1,0:T(8,128)}, u32[]{:S(2)}) copy-start(f32[256,768]{1,0:T(8,128)} %all-reduce.5.cloned.1.call-done) | copy-start | bytes 2359300
  100.1 44.9 %copy-start.3 = (bf16[4,32,1024]{2,1,0:T(8,128)(2,1)S(1)}, bf16[4,32,1024]{2,1,0:T(8,128)(2,1)}, u32[]{:S(2)}) copy-start(bf16[4,32,1024]{2,1,0:T(8,128)(2,1)} %param.25) | copy-start | bytes 786436
Sparse Core Ops, SparseCore 0:
  26.2 22.2 all-gather.2
  51.6 43.9 all-reduce.4
  146.9 25.7 reduce-scatter.1
where the time goes:
time: 181 us
  blocking collectives  91.1 us (50%)
  waiting for transfers between devices  64.2 us (35%)
  between operations  13.4 us (7%)
  matrix products  9.89 us (5%)
    reduce_scatter x1, waiting for transfers between devices, shards(): out = lax.psum_scatter(out, 'wide', scatter_dimension=0, tiled=True)  25.9 us
    psum x1, blocking collectives, shards(): mixed = lax.psum(mixed, 'wide').astype(bf16)  25.1 us
    all_gather x1, waiting for transfers between devices, shards(): full = lax.all_gather(rows, 'narrow', axis=1, tiled=True)  22.3 us
    all_gather x1, blocking collectives, shards(): rows = lax.all_gather(tokens, 'wide', axis=0, tiled=True)  19.5 us
    psum x1, waiting for transfers between devices, shards(): both = lax.psum(dot32(part, base_both), 'wide')  15.9 us
    psum x1, blocking collectives, shards(): lax.psum(jnp.einsum('td,edr->ter', rows, lefts, preferred_element_type=jn...  13.8 us
    all_gather x1, blocking collectives, shards(): weights = lax.all_gather(weight_of, 'wide', axis=0, tiled=True)  13.5 us
    psum x1, blocking collectives, shards(): thin = lax.psum(jnp.concatenate(thin, axis=1), 'narrow').astype(bf16)  11.8 us
  transfers between devices with their start and end apart: 3, of which 3 were waited for; matrix products, arithmetic and copies ran while one was open for 0% of the time, Pallas kernels for 0%

commit v1 on v0

--- a/solution.py
+++ b/solution.py
@@ -40,7 +40,7 @@
     depth = base_gate.shape[0]
     part = lax.dynamic_slice_in_dim(full, mine * depth, depth, axis=1)
     base_both = jnp.concatenate([base_gate, base_up], axis=1)
-    both = lax.psum(dot32(part, base_both), "wide")
+    both = jnp.sum(lax.all_gather(dot32(part, base_both), "wide"), axis=0)
     columns = base_gate.shape[1]
     lefts = jnp.concatenate([gate_left, up_left], axis=0)
     low = lax.psum(

time: 181 us -> 201 us (1.11)
  waiting for transfers between devices: 64.2 us -> 83.1 us
  other arithmetic: 1.75 us -> 3.95 us
  matrix products: 9.89 us -> 7.8 us
    all_gather x0 -> x1, waiting for transfers between devices: none -> 35 us  [shards(): both = jnp.sum(lax.all_gather(dot32(part, base_both), 'wide'), axis=0)]
    psum x1 -> x0, waiting for transfers between devices: 15.9 us -> none  [shards(): both = lax.psum(dot32(part, base_both), 'wide')]
    reduce_sum x0 -> x1, other arithmetic: none -> 2.2 us  [shards(): both = jnp.sum(lax.all_gather(dot32(part, base_both), 'wide'), axis=0)]
    dot_general x15, matrix products: 9.54 us -> 7.46 us  [dot32(): return jnp.dot(a, b, preferred_element_type=jnp.float32)]
where the time goes in v1:
time: 201 us
  blocking collectives  91.8 us (46%)
  waiting for transfers between devices  83.1 us (41%)
  between operations  13.4 us (7%)
  matrix products  7.8 us (4%)
  other arithmetic  3.95 us (2%)
    all_gather x1, waiting for transfers between devices, shards(): both = jnp.sum(lax.all_gather(dot32(part, base_both), 'wide'), axis=0)  35 us
    reduce_scatter x1, waiting for transfers between devices, shards(): out = lax.psum_scatter(out, 'wide', scatter_dimension=0, tiled=True)  25.7 us
    psum x1, blocking collectives, shards(): mixed = lax.psum(mixed, 'wide').astype(bf16)  23.1 us
    all_gather x1, waiting for transfers between devices, shards(): full = lax.all_gather(rows, 'narrow', axis=1, tiled=True)  22.4 us
    all_gather x1, blocking collectives, shards(): rows = lax.all_gather(tokens, 'wide', axis=0, tiled=True)  19.5 us
    psum x1, blocking collectives, shards(): lax.psum(jnp.einsum('td,edr->ter', rows, lefts, preferred_element_type=jn...  14.6 us
    all_gather x1, blocking collectives, shards(): weights = lax.all_gather(weight_of, 'wide', axis=0, tiled=True)  13.2 us
    psum x1, blocking collectives, shards(): thin = lax.psum(jnp.concatenate(thin, axis=1), 'narrow').astype(bf16)  12.7 us
  transfers between devices with their start and end apart: 3, of which 3 were waited for; matrix products, arithmetic and copies ran while one was open for 0% of the time, Pallas kernels for 0%

profile of v1, /device:TPU:0, one launch (start us, length us, event | category | flops | bytes accessed | tf_op | source)
XLA Modules:
  0.0 200.8 jit_solution(4705600167929006232)
XLA Ops:
  6.5 0.0 copy-start
  6.5 0.0 all-gather.5.cloned.1.call-start
  6.5 19.5 %all_gather.18 = bf16[256,1024]{1,0:T(8,128)(2,1)} all-gather(bf16[64,1024]{1,0:T(8,128)(2,1)} %param.13), channel_id=1, replica_groups=mesh['groups'=2,'wide'=4,'narrow'=4] {'wide'}, dimensions={0}, use_global_device_ids=true | all-gather | bytes 655360 | tf_op jit(solution)/shard_map/all_gather | solution.py:38
  26.0 0.0 all-gather.5.cloned.1.call-update
  26.0 0.0 all-gather.7.cloned.1.call-start
  26.1 0.0 copy-start.1
  26.1 0.0 copy-start.9
  26.1 0.0 copy-start.10
  26.1 22.4 %all-gather.5.cloned.1.call-done = bf16[256,4096]{1,0:T(8,128)(2,1)} async-done(((bf16[256,1024]{1,0:T(8,128)(2,1)}), bf16[256,4096]{1,0:T(8,128)(2,1)}) %all-gather.5.cloned.1.call-update) | async-done | bytes 2097168 | tf_op jit(solution)/shard_map/all_gather | solution.py:39
  48.5 3.0 %fusion = f32[256,768]{1,0:T(8,128)} fusion(bf16[1024,384]{1,0:T(8,128)(2,1)} %param.18, bf16[1024,384]{1,0:T(8,128)(2,1)} %param.17, bf16[256,4096]{1,0:T(8,128)(2,1)} %all-gather.5.cloned.1.call-done, s32[]{:T(128)S(6)} %select_n.17), kind=kOutput, calls=%fused_computation | convolution fusion | flops 405798912 | bytes 2883588 | tf_op jit(solution)/shard_map/dot_general | solution.py:8
  51.4 0.0 copy-start.6
  51.5 0.0 copy-start.8
  51.5 0.0 copy-start.7
  51.5 0.0 all-gather.7.cloned.1.call-update
  51.5 0.0 reduce-scatter.2.cloned.1.call-start
  51.5 0.0 copy-done.1
  51.5 0.0 copy-done.9
  51.5 0.0 copy-done.10
  51.6 0.3 convolution_bitcast_fusion
  51.9 0.2 copy-done.6
  52.1 0.0 copy-done.8
  52.1 0.1 select_reduce_fusion.1
  52.2 0.0 copy-done.7
  52.3 13.2 %all-gather.1 = f32[4,64,16]{1,2,0:T(8,128)S(1)} all-gather(f32[1,64,16]{1,2,0:T(8,128)S(1)} %bitcast.84), channel_id=1, replica_groups=mesh['groups'=2,'wide'=4,'narrow'=4] {'wide'}, dimensions={0}, use_global_device_ids=true | all-gather | bytes 20480 | tf_op jit(solution)/shard_map/all_gather | solution.py:36
  65.5 0.1 reshape.10
  65.6 0.0 copy-start.3
  65.6 14.6 %all-reduce.3 = bf16[256,8,32]{0,2,1:T(8,128)(2,1)S(1)} all-reduce(f32[256,8,32]{0,2,1:T(8,128)S(1)} %convolution_bitcast_fusion), channel_id=1, replica_groups=mesh['groups'=2,'wide'=4,'narrow'=4] {'narrow'}, use_global_device_ids=true, to_apply=%region_1.2 | all-reduce | flops 65536 | bytes 393216 | tf_op jit(solution)/shard_map/psum | solution.py:46
  80.2 35.0 %all-gather.7.cloned.1.call-done = f32[1024,768]{1,0:T(8,128)} async-done(((f32[256,768]{1,0:T(8,128)}), f32[1024,768]{1,0:T(8,128)}) %all-gather.7.cloned.1.call-update) | async-done | bytes 3145744 | tf_op jit(solution)/shard_map/all_gather | solution.py:43
  115.2 2.2 %reduce_sum.27 = f32[256,768]{1,0:T(8,128)S(1)} reduce(f32[4,256,768]{2,1,0:T(8,128)} %bitcast.82, f32[]{:T(128)} %constant.21.clone.1), dimensions={0}, to_apply=%region_0.1 | reduce | flops 589824 | bytes 3932164 | tf_op jit(solution)/shard_map/reduce_sum | solution.py:43
  117.4 0.0 copy-done.3
  117.4 0.0 copy-start.5
  117.4 0.2 convolution_add_fusion.4
  117.6 0.2 convolution_add_fusion.8
  117.9 0.2 convolution_add_fusion.6
  118.1 0.2 convolution_add_fusion.2
  118.4 0.0 copy-done.5
  118.4 0.0 copy-start.4
  118.4 0.3 fusion.10
  118.7 0.3 fusion.9
  118.9 0.3 copy-done.4
  119.3 0.2 fusion.19
  119.4 0.2 fusion.21
  119.6 0.3 fusion.8
  119.9 0.2 fusion.23
  120.1 0.0 copy-start.2
  120.1 0.3 add_add_fusion
  120.4 0.2 fusion.17
  120.6 12.7 %all-reduce.4 = bf16[256,128]{0,1:T(8,128)(2,1)S(1)} all-reduce(f32[256,128]{0,1:T(8,128)S(1)} %pad_maximum_fusion), channel_id=1, replica_groups=mesh['groups'=2,'wide'=4,'narrow'=4] {'narrow'}, use_global_device_ids=true, to_apply=%region_5.6 | all-reduce | flops 32768 | bytes 196608 | tf_op jit(solution)/shard_map/psum | solution.py:62
  133.3 23.1 %all-reduce.5 = bf16[256,384]{1,0:T(8,128)(2,1)S(1)} all-reduce(f32[256,384]{1,0:T(8,128)S(1)} %get-tuple-element.9), channel_id=1, replica_groups=mesh['groups'=2,'wide'=4,'narrow'=4] {'wide'}, use_global_device_ids=true, to_apply=%region_4.5 | all-reduce | flops 98304 | bytes 589824 | tf_op jit(solution)/shard_map/psum | solution.py:58
  156.4 8.8 %all_gather.23 = bf16[256,1536]{1,0:T(8,128)(2,1)S(1)} all-gather(bf16[256,384]{1,0:T(8,128)(2,1)S(1)} %all-reduce.5), channel_id=1, replica_groups=mesh['groups'=2,'wide'=4,'narrow'=4] {'narrow'}, dimensions={1}, use_global_device_ids=true | all-gather | bytes 983040 | tf_op jit(solution)/shard_map/all_gather | solution.py:59
  165.2 0.0 copy-done.2
  165.2 0.3 fusion.56
  165.5 0.0 copy-done
  165.6 1.4 convolution_add_fusion
  167.0 0.0 reduce-scatter.2.cloned.1.call-update
  167.0 25.7 %reduce-scatter.2.cloned.1.call-done = f32[64,1024]{1,0:T(8,128)} async-done(((f32[256,1024]{1,0:T(8,128)}), f32[64,1024]{1,0:T(8,128)}) %reduce-scatter.2.cloned.1.call-update) | async-done | bytes 262160 | tf_op jit(solution)/shard_map/reduce_scatter | solution.py:64
  192.7 1.6 convert_element_type.31
  (4 shorter events, 0.1 us)
Async XLA Ops:
  6.5 159.0 %copy-start = (bf16[384,1024]{1,0:T(8,128)(2,1)S(1)}, bf16[384,1024]{1,0:T(8,128)(2,1)}, u32[]{:S(2)}) copy-start(bf16[384,1024]{1,0:T(8,128)(2,1)} %param.19) | copy-start | bytes 2359300
  6.5 41.9 %all-gather.5.cloned.1.call-start = ((), (), s32[]{:S(2)}) async-start(), calls=%async_computation.1 | async-start | bytes 2621440 | tf_op jit(solution)/shard_map/all_gather | solution.py:39
  26.0 89.1 %all-gather.7.cloned.1.call-start = ((), (), s32[]{:S(2)}) async-start(), calls=%async_computation.3 | async-start | bytes 3932160 | tf_op jit(solution)/shard_map/all_gather | solution.py:43
  26.1 25.4 %copy-start.1 = (bf16[256,1024]{1,0:T(8,128)(2,1)S(1)}, bf16[256,1024]{1,0:T(8,128)(2,1)}, u32[]{:S(2)}) copy-start(bf16[256,1024]{1,0:T(8,128)(2,1)} %all_gather.18) | copy-start | bytes 1572868
  26.1 25.4 %copy-start.9 = (bf16[4,1024,32]{1,2,0:T(8,128)(2,1)S(1)}, bf16[4,1024,32]{1,2,0:T(8,128)(2,1)}, u32[]{:S(2)}) copy-start(bf16[4,1024,32]{1,2,0:T(8,128)(2,1)} %param.22) | copy-start | bytes 786436
  26.1 25.4 %copy-start.10 = (bf16[4,1024,32]{1,2,0:T(8,128)(2,1)S(1)}, bf16[4,1024,32]{1,2,0:T(8,128)(2,1)}, u32[]{:S(2)}) copy-start(bf16[4,1024,32]{1,2,0:T(8,128)(2,1)} %param.20) | copy-start | bytes 786436
  51.4 0.7 copy-start.6
  51.5 0.7 copy-start.8
  51.5 0.8 copy-start.7
  51.5 141.2 %reduce-scatter.2.cloned.1.call-start = ((), (), s32[]{:S(2)}) async-start(), calls=%async_computation.2 | async-start | bytes 1310720 | tf_op jit(solution)/shard_map/reduce_scatter | solution.py:64
  65.6 51.7 %copy-start.3 = (bf16[4,32,384]{2,1,0:T(8,128)(2,1)S(1)}, bf16[4,32,384]{2,1,0:T(8,128)(2,1)}, u32[]{:S(2)}) copy-start(bf16[4,32,384]{2,1,0:T(8,128)(2,1)} %param.21) | copy-start | bytes 294916
  117.4 1.0 copy-start.5
  118.4 0.9 copy-start.4
  120.1 45.1 %copy-start.2 = (bf16[4,32,1024]{2,1,0:T(8,128)(2,1)S(1)}, bf16[4,32,1024]{2,1,0:T(8,128)(2,1)}, u32[]{:S(2)}) copy-start(bf16[4,32,1024]{2,1,0:T(8,128)(2,1)} %param.25) | copy-start | bytes 786436
Sparse Core Ops, SparseCore 0:
  26.1 22.2 all-gather.4
  51.6 63.5 all-gather.6
  167.1 25.5 reduce-scatter.1
